TPU v7x, 32 devices: a whole 2x2x4 slice. The times are simulated.
32 devices in a mesh: grp: 4 (over y, x), mem: 8 (over z, core).
Axes of the slice: x: 2, y: 2, z: 4, core: 2. Of those that a mesh axis runs over, the one named last changes fastest.
Arguments:
- points: float32 [512, 128], P(('grp', 'mem')), may hold values from -40 to 40, as said below
- slab: float32 [16384, 128], P('mem'), may hold values from -40 to 40, as said below
Outputs:
- new_points: float32 [512, 128], P(('grp', 'mem'))
Inputs may be any that keep to these rules, and one draw needn't show every extreme that they name: Support points lie near the chains' centres. `slab`: each block of 2048 rows is one chain with its own centre and scale.
All inputs are finite; a program needn't handle non-finite values.
Results may differ from a plain program's by a relative error of at most 0.0001.
Values sent between devices are 32-bit elements; how exact they have to be, the bound alone decides.
A program may use at most 64 MiB of HBM per device.

v0:
```python
import jax
import jax.numpy as jnp
from jax import lax
from jax.sharding import PartitionSpec as P


def weights_of(left, right_operand):
    left_square_norm = jnp.sum(jnp.square(left), axis=1)
    right_square_norm = jnp.sum(jnp.square(right_operand), axis=1)
    cross_product = jnp.dot(
        left, right_operand.T, precision=lax.Precision.HIGHEST, preferred_element_type=jnp.float32
    )
    squared_distance = left_square_norm[:, None] + right_square_norm[None, :] - 2.0 * cross_product
    return 1.0 / jnp.sqrt(squared_distance + 1.0)


def pair_terms(anchors, piece):
    wts = weights_of(anchors, piece)
    pair_vec = jnp.dot(
        wts, piece, precision=lax.Precision.HIGHEST, preferred_element_type=jnp.float32
    )
    pair_sum = jnp.sum(wts, axis=1)
    return (pair_vec, pair_sum)


def shards(points, slab):
    owned = points.shape[0]
    width = points.shape[1]
    samp_rows = slab.shape[0]
    groups = lax.axis_size("grp")
    ratio = samp_rows / (owned * groups)
    group = lax.all_gather(points, "mem", axis=0, tiled=True)
    sblock = min(samp_rows, 512)
    slab_blocks = slab.reshape(samp_rows // sblock, sblock, width)

    def attract_step(carry, rows):
        numer, total = carry
        wts = weights_of(group, rows)
        numer = numer + jnp.dot(
            wts, rows, precision=lax.Precision.HIGHEST, preferred_element_type=jnp.float32
        )
        total = total + jnp.sum(wts, axis=1)
        return ((numer, total), None)

    init = (
        jnp.zeros((group.shape[0], width), jnp.float32),
        jnp.zeros((group.shape[0],), jnp.float32),
    )
    (numer, total), _ = lax.scan(attract_step, init, slab_blocks)
    numer_all, total_all = lax.psum((numer, total), "mem")
    first = lax.axis_index("mem") * owned
    numer_own = lax.dynamic_slice_in_dim(numer_all, first, owned, 0)
    total_own = lax.dynamic_slice_in_dim(total_all, first, owned, 0)
    pair_vec, pair_sum = pair_terms(points, lax.all_gather(group, "grp", axis=0, tiled=True))
    repel = points * pair_sum[:, None] - pair_vec
    update_output = (ratio * repel + numer_own) / total_own[:, None]
    return update_output


def solution(mesh):
    placed = (P(("grp", "mem"), None), P("mem", None))
    return jax.shard_map(
        shards, mesh=mesh, in_specs=placed, out_specs=P(("grp", "mem"), None), check_vma=False
    )
```

profile of v0, /device:TPU:0, one launch (start us, length us, event | category | flops | bytes accessed | tf_op | source)
XLA Modules:
  0.0 103.8 jit_solution(17931212390911366223)
XLA Ops:
  6.5 15.9 %all_gather.6 = f32[128,128]{1,0:T(8,128)S(1)} all-gather(f32[16,128]{1,0:T(8,128)} %param.4), channel_id=1, replica_groups=mesh['grp'=4,'mem'=8] {'mem'}, dimensions={0}, use_global_device_ids=true | all-gather | bytes 73728 | tf_op jit(solution)/shard_map/all_gather | solution.py:32
  22.4 0.1 multiply_reduce_fusion.1
  22.5 16.2 %while.15 = (s32[]{:T(128)}, f32[128,128]{1,0:T(8,128)S(1)}, f32[128]{0:T(128)S(1)}, f32[128]{0:T(128)S(1)}, f32[4,512,128]{2,1,0:T(8,128)}, /*index=5*/f32[128,128]{1,0:T(8,128)S(1)}, s32[]{:T(128)}, s32[]{:T(128)}) while((s32[]{:T(128)}, f32[128,128]{1,0:T(8,128)S(1)}, f32[128]{0:T(128)S(1)}, f32[128]{0:T(128)S(1)}, ...), condition=%wide.region_7.8_spmd.clone, body=%wide.region_4.7_spmd.clone.sunk | while | flops 201817728 | bytes 1515108 | solution.py:49
  22.5 1.1 %fusion.35 = f32[512]{0:T(512)S(1)} fusion(f32[4,512,128]{2,1,0:T(8,128)} %get-tuple-element.172, s32[]{:T(128)} %get-tuple-element.160), kind=kLoop, calls=%fused_computation.9.clone.1 | loop fusion | flops 130560 | bytes 264196 | tf_op jit(solution)/shard_map/while/body/eval_jaxpr/reduce_sum | solution.py:9
  23.6 1.4 %fusion.36 = (f32[128]{0:T(128)S(1)}, f32[128,512]{0,1:T(8,128)S(1)}) fusion(f32[128,128]{1,0:T(8,128)S(1)} %get-tuple-element.173, f32[4,512,128]{2,1,0:T(8,128)} %get-tuple-element.172, s32[]{:T(128)} %get-tuple-element.160, f32[512]{0:T(512)S(1)} %fusion.35, f32[128]{0:T(128)S(1)} %get-tuple-element.171), kind=kOutput, calls=%fused_computation.27.clone.1 | convolution fusion | flops 100990848 | bytes 593408 | tf_op jit(solution)/shard_map/while/body/eval_jaxpr/dot_general | solution.py:10
  25.0 1.6 %convolution_add_fusion.2 = f32[128,128]{1,0:T(8,128)S(1)} fusion(f32[128,512]{0,1:T(8,128)S(1)} %get-tuple-element.150, f32[4,512,128]{2,1,0:T(8,128)} %get-tuple-element.172, s32[]{:T(128)} %get-tuple-element.160, f32[128,128]{1,0:T(8,128)S(1)} %get-tuple-element.161, pred[]{:T(512)S(6)} %compare.3), kind=kOutput, calls=%fused_computation.5.clone.1 | convolution fusion | flops 100696064 | bytes 655873 | tf_op jit(solution)/shard_map/while/body/eval_jaxpr/dot_general | solution.py:39
  26.6 1.1 %fusion.35 = f32[512]{0:T(512)S(1)} fusion(f32[4,512,128]{2,1,0:T(8,128)} %get-tuple-element.172, s32[]{:T(128)} %get-tuple-element.160), kind=kLoop, calls=%fused_computation.9.clone.1 | loop fusion | flops 130560 | bytes 264196 | tf_op jit(solution)/shard_map/while/body/eval_jaxpr/reduce_sum | solution.py:9
  27.7 1.4 %fusion.36 = (f32[128]{0:T(128)S(1)}, f32[128,512]{0,1:T(8,128)S(1)}) fusion(f32[128,128]{1,0:T(8,128)S(1)} %get-tuple-element.173, f32[4,512,128]{2,1,0:T(8,128)} %get-tuple-element.172, s32[]{:T(128)} %get-tuple-element.160, f32[512]{0:T(512)S(1)} %fusion.35, f32[128]{0:T(128)S(1)} %get-tuple-element.171), kind=kOutput, calls=%fused_computation.27.clone.1 | convolution fusion | flops 100990848 | bytes 593408 | tf_op jit(solution)/shard_map/while/body/eval_jaxpr/dot_general | solution.py:10
  29.1 1.6 %convolution_add_fusion.2 = f32[128,128]{1,0:T(8,128)S(1)} fusion(f32[128,512]{0,1:T(8,128)S(1)} %get-tuple-element.150, f32[4,512,128]{2,1,0:T(8,128)} %get-tuple-element.172, s32[]{:T(128)} %get-tuple-element.160, f32[128,128]{1,0:T(8,128)S(1)} %get-tuple-element.161, pred[]{:T(512)S(6)} %compare.3), kind=kOutput, calls=%fused_computation.5.clone.1 | convolution fusion | flops 100696064 | bytes 655873 | tf_op jit(solution)/shard_map/while/body/eval_jaxpr/dot_general | solution.py:39
  30.7 1.1 %fusion.35 = f32[512]{0:T(512)S(1)} fusion(f32[4,512,128]{2,1,0:T(8,128)} %get-tuple-element.172, s32[]{:T(128)} %get-tuple-element.160), kind=kLoop, calls=%fused_computation.9.clone.1 | loop fusion | flops 130560 | bytes 264196 | tf_op jit(solution)/shard_map/while/body/eval_jaxpr/reduce_sum | solution.py:9
  31.8 1.4 %fusion.36 = (f32[128]{0:T(128)S(1)}, f32[128,512]{0,1:T(8,128)S(1)}) fusion(f32[128,128]{1,0:T(8,128)S(1)} %get-tuple-element.173, f32[4,512,128]{2,1,0:T(8,128)} %get-tuple-element.172, s32[]{:T(128)} %get-tuple-element.160, f32[512]{0:T(512)S(1)} %fusion.35, f32[128]{0:T(128)S(1)} %get-tuple-element.171), kind=kOutput, calls=%fused_computation.27.clone.1 | convolution fusion | flops 100990848 | bytes 593408 | tf_op jit(solution)/shard_map/while/body/eval_jaxpr/dot_general | solution.py:10
  33.1 1.6 %convolution_add_fusion.2 = f32[128,128]{1,0:T(8,128)S(1)} fusion(f32[128,512]{0,1:T(8,128)S(1)} %get-tuple-element.150, f32[4,512,128]{2,1,0:T(8,128)} %get-tuple-element.172, s32[]{:T(128)} %get-tuple-element.160, f32[128,128]{1,0:T(8,128)S(1)} %get-tuple-element.161, pred[]{:T(512)S(6)} %compare.3), kind=kOutput, calls=%fused_computation.5.clone.1 | convolution fusion | flops 100696064 | bytes 655873 | tf_op jit(solution)/shard_map/while/body/eval_jaxpr/dot_general | solution.py:39
  34.7 1.1 %fusion.35 = f32[512]{0:T(512)S(1)} fusion(f32[4,512,128]{2,1,0:T(8,128)} %get-tuple-element.172, s32[]{:T(128)} %get-tuple-element.160), kind=kLoop, calls=%fused_computation.9.clone.1 | loop fusion | flops 130560 | bytes 264196 | tf_op jit(solution)/shard_map/while/body/eval_jaxpr/reduce_sum | solution.py:9
  35.8 1.4 %fusion.36 = (f32[128]{0:T(128)S(1)}, f32[128,512]{0,1:T(8,128)S(1)}) fusion(f32[128,128]{1,0:T(8,128)S(1)} %get-tuple-element.173, f32[4,512,128]{2,1,0:T(8,128)} %get-tuple-element.172, s32[]{:T(128)} %get-tuple-element.160, f32[512]{0:T(512)S(1)} %fusion.35, f32[128]{0:T(128)S(1)} %get-tuple-element.171), kind=kOutput, calls=%fused_computation.27.clone.1 | convolution fusion | flops 100990848 | bytes 593408 | tf_op jit(solution)/shard_map/while/body/eval_jaxpr/dot_general | solution.py:10
  37.2 1.6 %convolution_add_fusion.2 = f32[128,128]{1,0:T(8,128)S(1)} fusion(f32[128,512]{0,1:T(8,128)S(1)} %get-tuple-element.150, f32[4,512,128]{2,1,0:T(8,128)} %get-tuple-element.172, s32[]{:T(128)} %get-tuple-element.160, f32[128,128]{1,0:T(8,128)S(1)} %get-tuple-element.161, pred[]{:T(512)S(6)} %compare.3), kind=kOutput, calls=%fused_computation.5.clone.1 | convolution fusion | flops 100696064 | bytes 655873 | tf_op jit(solution)/shard_map/while/body/eval_jaxpr/dot_general | solution.py:39
  38.8 0.6 copy-done
  39.4 9.0 %all_gather.7 = f32[512,128]{1,0:T(8,128)S(1)} all-gather(f32[128,128]{1,0:T(8,128)S(1)} %get-tuple-element.177), channel_id=1, replica_groups=mesh['grp'=4,'mem'=8] {'grp'}, dimensions={0}, use_global_device_ids=true | all-gather | bytes 327680 | tf_op jit(solution)/shard_map/all_gather | solution.py:54
  48.4 0.1 multiply_reduce_fusion.2
  48.5 0.1 multiply_reduce_fusion
  48.7 0.4 fusion.19
  49.1 14.9 %psum.15 = f32[128]{0:T(128)S(1)} all-reduce(f32[128]{0:T(128)S(1)} %get-tuple-element.73), channel_id=1, replica_groups=mesh['grp'=4,'mem'=8] {'mem'}, use_global_device_ids=true, to_apply=%region_9.10 | all-reduce | flops 128 | bytes 1024 | tf_op jit(solution)/shard_map/psum | solution.py:50
  64.0 0.1 dynamic_slice.13
  64.1 31.3 %all-reduce.2.cloned.1.call-done = f32[128,128]{1,0:T(8,128)} async-done(((f32[128,128]{1,0:T(8,128)}), f32[128,128]{1,0:T(8,128)}) %all-reduce.2.cloned.1.call-update) | async-done | bytes 65552 | tf_op jit(solution)/shard_map/psum | solution.py:50
  95.4 1.5 %fusion.17 = f32[16,128]{1,0:T(8,128)} fusion(f32[16,512]{1,0:T(8,128)S(1)} %get-tuple-element.110, f32[512,128]{1,0:T(8,128)S(1)} %all_gather.7, f32[128,128]{1,0:T(8,128)} %all-reduce.2.cloned.1.call-done, s32[]{:T(128)S(6)} %select_n.4, f32[16,128]{1,0:T(8,128)S(1)} %copy-done.1, f32[16]{0:T(128)S(1)} %dynamic_slice.13, f32[16]{0:T(128)S(1)} %get-tuple-element.109), kind=kOutput, calls=%fused_computation.23 | convolution fusion | flops 12593152 | bytes 319620 | tf_op jit(solution)/shard_map/dot_general | solution.py:19
  (11 shorter events, 0.1 us)
Async XLA Ops:
  6.5 88.8 %all-reduce.2.cloned.1.call-start = ((), (), s32[]{:S(2)}) async-start(), calls=%async_computation | async-start | bytes 131072 | tf_op jit(solution)/shard_map/psum | solution.py:50
  38.8 0.6 copy-start
  39.4 9.0 %copy-start.1 = (f32[16,128]{1,0:T(8,128)S(1)}, f32[16,128]{1,0:T(8,128)}, u32[]{:S(2)}) copy-start(f32[16,128]{1,0:T(8,128)} %param.4) | copy-start | bytes 24580
Sparse Core Ops, SparseCore 0:
  39.5 55.7 all-reduce.1
where the time goes:
time: 104 us
  blocking collectives  39.8 us (38%)
  waiting for transfers between devices  31.3 us (30%)
  matrix products  13.7 us (13%)
  between operations  13.4 us (13%)
  other arithmetic  4.8 us (5%)
    psum x1, waiting for transfers between devices, shards(): numer_all, total_all = lax.psum((numer, total), 'mem')  31.3 us
    all_gather x1, blocking collectives, shards(): group = lax.all_gather(points, 'mem', axis=0, tiled=True)  15.9 us
    psum x1, blocking collectives, shards(): numer_all, total_all = lax.psum((numer, total), 'mem')  14.9 us
    all_gather x1, blocking collectives, shards(): lax.all_gather(group, 'grp', axis=0, tiled=True)  8.99 us
    dot_general x4, matrix products, attract_step(): jnp.dot(wts, rows, precision=lax.Precision.HIGHEST, preferred_element_typ...  6.21 us
    dot_general x5, matrix products, weights_of(): jnp.dot(left, right_operand.T, precision=lax.Precision.HIGHEST, preferred...  5.89 us
    reduce_sum x5, other arithmetic, weights_of(): right_square_norm = jnp.sum(jnp.square(right_operand), axis=1)  4.54 us
  transfers between devices with their start and end apart: 1, of which 1 were waited for; matrix products, arithmetic and copies ran while one was open for 1% of the time, Pallas kernels for 0%

commit v1 on v0

v1 whole, which is shorter than its diff:
```python
import functools

import jax
import jax.numpy as jnp
from jax import lax
from jax.experimental import pallas as pl
from jax.experimental.pallas import tpu as pltpu
from jax.sharding import PartitionSpec as P

MESH = pl.DeviceIdType.MESH
NT = (((1,), (1,)), ((), ()))
LANES = 128


def split3(x):
    hi = x.astype(jnp.bfloat16)
    rest = x - hi.astype(jnp.float32)
    mid = rest.astype(jnp.bfloat16)
    low = (rest - mid.astype(jnp.float32)).astype(jnp.bfloat16)
    return hi, mid, low


def split2(x):
    hi = x.astype(jnp.bfloat16)
    return hi, (x - hi.astype(jnp.float32)).astype(jnp.bfloat16)


def ndot(left, right):
    return lax.dot_general(left, right, NT, preferred_element_type=jnp.float32)


def prep_rows(rows):
    hi, mid, low = split3(rows)
    q1, q2, q3 = split3(rows * rows)
    ones = jnp.ones((8, rows.shape[1]), jnp.bfloat16)
    norm = ndot(ones, q1) + (ndot(ones, q2) + ndot(ones, q3))
    return (
        jnp.concatenate([hi, mid], axis=1),
        jnp.concatenate([low, hi], axis=1),
        norm,
    )


def kernel(
    ng, nm, ratio, chunk,
    pts_hbm, slab_hbm, out_ref,
    gp, cp, slab_v, b12, b31, bn, sendbuf, recvbuf,
    loc_sem, slab_sem, gsend, grecv, csend, crecv, rsend, rrecv,
):
    g = lax.axis_index("grp")
    m = lax.axis_index("mem")
    owned, width = pts_hbm.shape
    rows = slab_hbm.shape[0]
    n_chunk = rows // chunk
    mem_peer = [lax.rem(m + j, nm) for j in range(nm)]
    grp_peer = [lax.rem(g + j, ng) for j in range(ng)]

    barrier = pltpu.get_barrier_semaphore()
    for j in range(1, nm):
        pl.semaphore_signal(barrier, inc=1, device_id=(g, mem_peer[j]), device_id_type=MESH)
    for j in range(1, ng):
        pl.semaphore_signal(barrier, inc=1, device_id=(grp_peer[j], m), device_id_type=MESH)

    own_g = pltpu.make_async_copy(pts_hbm, gp.at[m], loc_sem.at[0])
    own_c = pltpu.make_async_copy(pts_hbm, cp.at[g], loc_sem.at[1])
    own_g.start()
    own_c.start()
    slab_copies = []
    for c in range(n_chunk):
        part = pl.ds(c * chunk, chunk)
        copy = pltpu.make_async_copy(slab_hbm.at[part], slab_v.at[part], slab_sem.at[c])
        copy.start()
        slab_copies.append(copy)
    pad = cp.shape[0] - ng
    if pad:
        cp[pl.ds(ng, pad)] = jnp.zeros((pad, owned, width), jnp.float32)

    own_g.wait()
    own_c.wait()
    pl.semaphore_wait(barrier, nm + ng - 2)

    sends = []
    for j in range(1, nm):
        copy = pltpu.make_async_remote_copy(
            src_ref=gp.at[m], dst_ref=gp.at[m],
            send_sem=gsend.at[j], recv_sem=grecv.at[j],
            device_id=(g, mem_peer[j]), device_id_type=MESH,
        )
        copy.start()
        sends.append(copy)
    for j in range(1, ng):
        copy = pltpu.make_async_remote_copy(
            src_ref=cp.at[g], dst_ref=cp.at[g],
            send_sem=csend.at[j], recv_sem=crecv.at[j],
            device_id=(grp_peer[j], m), device_id_type=MESH,
        )
        copy.start()
        sends.append(copy)

    for c in range(n_chunk):
        part = pl.ds(c * chunk, chunk)
        slab_copies[c].wait()
        b12[part], b31[part], bn[:, part] = prep_rows(slab_v[part])

    for copy in sends:
        copy.wait_recv()

    pts = gp[...].reshape(nm * owned, width)
    count = nm * owned
    norm1 = jnp.sum(pts * pts, axis=1, keepdims=True) + 1.0
    p1, p2, p3 = split3(-2.0 * pts)
    left12 = jnp.concatenate(
        [jnp.concatenate([p1, p1], axis=1), jnp.concatenate([p2, p2], axis=1)], axis=0
    )
    left31 = jnp.concatenate([p1, p3], axis=1)

    def weights(r12, r31, norms):
        both = ndot(left12, r12)
        cross = both[:count] + both[count:] + ndot(left31, r31)
        return lax.rsqrt(norm1 + norms + cross)

    def folded(w):
        total = w[:, :LANES]
        for k in range(1, w.shape[1] // LANES):
            total = total + w[:, k * LANES:(k + 1) * LANES]
        return total

    def accum(w, r12):
        return jnp.dot(
            jnp.concatenate(split2(w), axis=0), r12, preferred_element_type=jnp.float32
        )

    pair_rows = cp[...].reshape(cp.shape[0] * owned, width)
    r12, r31, norms = prep_rows(pair_rows)
    w = weights(r12, r31, norms[0:1])
    if pad:
        lane = lax.broadcasted_iota(jnp.int32, w.shape, 1)
        w = jnp.where(lane < ng * owned, w, 0.0)
    pair_part = folded(w)
    acc = accum(w * (-ratio), r12)
    weight_part = None
    for c in range(n_chunk):
        part = pl.ds(c * chunk, chunk)
        r12 = b12[part]
        w = weights(r12, b31[part], bn[0:1, part])
        weight_part = folded(w) if weight_part is None else weight_part + folded(w)
        acc = acc + accum(w, r12)
    acc = acc[:count] + acc[count:]
    acc = acc[:, :width] + acc[:, width:]
    weight_row = jnp.sum(weight_part.T, axis=0, keepdims=True)
    pair_row = jnp.sum(pair_part.T, axis=0, keepdims=True)
    for t in range(nm):
        seg = pl.ds((t * owned) // LANES * LANES, LANES)
        lo = (t * owned) // LANES * LANES
        sendbuf[t, 0:owned] = acc[t * owned:(t + 1) * owned]
        sendbuf[t, owned:owned + 1] = weight_row[:, lo:lo + LANES]
        sendbuf[t, owned + 1:owned + 2] = pair_row[:, lo:lo + LANES]

    outs = []
    for j in range(1, nm):
        copy = pltpu.make_async_remote_copy(
            src_ref=sendbuf.at[mem_peer[j], pl.ds(0, owned + 2)],
            dst_ref=recvbuf.at[j, pl.ds(0, owned + 2)],
            send_sem=rsend.at[j], recv_sem=rrecv.at[j],
            device_id=(g, mem_peer[j]), device_id_type=MESH,
        )
        copy.start()
        outs.append(copy)
    for copy in outs:
        copy.wait_recv()
    vec = sendbuf[m, 0:owned]
    sums = sendbuf[m, owned:owned + 2]
    for j in range(1, nm):
        vec = vec + recvbuf[j, 0:owned]
        sums = sums + recvbuf[j, owned:owned + 2]
    lane = lax.broadcasted_iota(jnp.int32, (owned, LANES), 1)
    row = lax.broadcasted_iota(jnp.int32, (owned, LANES), 0)
    mine = lane == row + lax.rem(m * owned, LANES)
    weight = jnp.sum(jnp.where(mine, sums[0:1], 0.0), axis=1, keepdims=True)
    pair = jnp.sum(jnp.where(mine, sums[1:2], 0.0), axis=1, keepdims=True)
    out_ref[...] = (gp[m] * (ratio * pair) + vec) / weight
    for copy in sends + outs:
        copy.wait_send()


def shards(points, slab):
    owned, width = points.shape
    rows = slab.shape[0]
    ng, nm = lax.axis_size("grp"), lax.axis_size("mem")
    ratio = rows / (owned * ng)
    chunk = min(rows, 512)
    n_chunk = rows // chunk
    pair_slots = -(-ng * owned // LANES) * LANES // owned
    sem = pltpu.SemaphoreType.DMA
    return pl.pallas_call(
        functools.partial(kernel, ng, nm, ratio, chunk),
        out_shape=jax.ShapeDtypeStruct((owned, width), jnp.float32),
        in_specs=[pl.BlockSpec(memory_space=pl.ANY)] * 2,
        out_specs=pl.BlockSpec(memory_space=pltpu.VMEM),
        scratch_shapes=[
            pltpu.VMEM((nm, owned, width), jnp.float32),
            pltpu.VMEM((pair_slots, owned, width), jnp.float32),
            pltpu.VMEM((rows, width), jnp.float32),
            pltpu.VMEM((rows, 2 * width), jnp.bfloat16),
            pltpu.VMEM((rows, 2 * width), jnp.bfloat16),
            pltpu.VMEM((8, rows), jnp.float32),
            pltpu.VMEM((nm, owned + 8, width), jnp.float32),
            pltpu.VMEM((nm, owned + 8, width), jnp.float32),
            sem((2,)), sem((n_chunk,)),
            sem((nm,)), sem((nm,)), sem((ng,)), sem((ng,)), sem((nm,)), sem((nm,)),
        ],
        compiler_params=pltpu.CompilerParams(collective_id=0, has_side_effects=True),
    )(points, slab)


def solution(mesh):
    placed = (P(("grp", "mem"), None), P("mem", None))
    return jax.shard_map(
        shards, mesh=mesh, in_specs=placed, out_specs=P(("grp", "mem"), None), check_vma=False
    )
```

time: 104 us -> 16.5 us (0.16)
  blocking collectives: 39.8 us -> 0 us
  waiting for transfers between devices: 31.3 us -> 0 us
  Pallas kernels: 0 us -> 15 us
  matrix products: 13.7 us -> 0 us
  between operations: 13.4 us -> 0.01 us
  other arithmetic: 4.8 us -> 0 us
    psum x1 -> x0, waiting for transfers between devices: 31.3 us -> none  [shards(): numer_all, total_all = lax.psum((numer, total), 'mem')]
    all_gather x2 -> x0, blocking collectives: 24.9 us -> none  [the longest x1 15.9 us: shards(): group = lax.all_gather(points, 'mem', axis=0, tiled=True)]
    pallas_call x0 -> x1, Pallas kernels: none -> 15 us  [shards(): pl.pallas_call(functools.partial(kernel, ng, nm, ratio, chunk), out_shape...]
    psum x1 -> x0, blocking collectives: 14.9 us -> none  [shards(): numer_all, total_all = lax.psum((numer, total), 'mem')]
    dot_general x10 -> x0, matrix products: 13.7 us -> none  [the longest x4 6.21 us: attract_step(): jnp.dot(wts, rows, precision=lax.Precision.HIGHEST, preferred_element_typ...]
    reduce_sum x7 -> x0, other arithmetic: 4.75 us -> none  [the longest x5 4.54 us: weights_of(): right_square_norm = jnp.sum(jnp.square(right_operand), axis=1)]
  transfers between devices with their start and end apart: 1 -> 0, of which waited for: 1 -> 0; matrix products, arithmetic and copies ran while one was open for 1% -> 0% of each run, Pallas kernels for 0% -> 0%
where the time goes in v1:
time: 16.5 us; the launch traced here: 16.3 us
  Pallas kernels  15 us (91%)
  local copies, waits for them, and re-layouts  1.3 us (8%)
    pallas_call x1, Pallas kernels, shards(): pl.pallas_call(functools.partial(kernel, ng, nm, ratio, chunk), out_shape...  15 us
    unnamed x1, local copies, waits for them, and re-layouts  1.3 us

profile of v1, /device:TPU:0, one launch (start us, length us, event | category | flops | bytes accessed | tf_op | source)
XLA Modules:
  0.0 16.3 jit_solution(14501003781244518639)
XLA Ops:
  0.0 15.0 %shard_map.28 = f32[16,128]{1,0:T(8,128)} custom-call(f32[16,128]{1,0:T(8,128)} %pts_hbm.1, f32[2048,128]{1,0:T(8,128)} %slab_hbm.1), custom_call_target="tpu_custom_call" | custom-call | tf_op jit(solution)/shard_map/pallas_call | solution.py:195
  15.0 1.3 %copy.4 = f32[16,128]{1,0:T(8,128)} copy(f32[16,128]{1,0:T(8,128)} %shard_map.28) | data formatting | bytes 16384

commit v2 on v1

v2 whole, which is shorter than its diff:
```python
import functools

import jax
import jax.numpy as jnp
from jax import lax
from jax.experimental import pallas as pl
from jax.experimental.pallas import tpu as pltpu
from jax.sharding import PartitionSpec as P

MESH = pl.DeviceIdType.MESH
NT = (((1,), (1,)), ((), ()))
LANES = 128
LEAD = 4


def split3(x):
    hi = x.astype(jnp.bfloat16)
    rest = x - hi.astype(jnp.float32)
    mid = rest.astype(jnp.bfloat16)
    low = (rest - mid.astype(jnp.float32)).astype(jnp.bfloat16)
    return hi, mid, low


def split2(x):
    hi = x.astype(jnp.bfloat16)
    return hi, (x - hi.astype(jnp.float32)).astype(jnp.bfloat16)


def ndot(left, right):
    return lax.dot_general(left, right, NT, preferred_element_type=jnp.float32)


def prep_rows(rows):
    hi, mid, low = split3(rows)
    q1, q2, q3 = split3(rows * rows)
    ones = jnp.ones((8, rows.shape[1]), jnp.bfloat16)
    norm = ndot(ones, q1) + (ndot(ones, q2) + ndot(ones, q3))
    return (
        jnp.concatenate([hi, mid], axis=1),
        jnp.concatenate([low, hi], axis=1),
        norm,
    )


def kernel(
    ng, nm, ratio, chunk,
    pts_hbm, slab_hbm, out_ref,
    gp, cp, slab_v, b12, b31, bn, sendbuf, recvbuf,
    loc_sem, slab_sem, ready, cready, gsend, grecv, psend, csend, crecv, rsend, rrecv,
):
    g = lax.axis_index("grp")
    m = lax.axis_index("mem")
    owned, width = pts_hbm.shape
    rows = slab_hbm.shape[0]
    n_chunk = rows // chunk
    mem_up = [jnp.minimum(m + j, nm - 1) for j in range(nm)]
    mem_down = [jnp.maximum(m - j, 0) for j in range(nm)]
    grp_up = [jnp.minimum(g + j, ng - 1) for j in range(ng)]
    grp_down = [jnp.maximum(g - j, 0) for j in range(ng)]
    odd = lax.rem(m, 2) == 1
    even = jnp.logical_not(odd)

    def both(*conds):
        return functools.reduce(jnp.logical_and, conds)

    def greet(semaphore, device):
        pl.semaphore_signal(semaphore, inc=1, device_id=device, device_id_type=MESH)

    barrier = pltpu.get_barrier_semaphore()
    for j in range(1, nm):
        pl.when(m + j < nm)(lambda j=j: greet(barrier, (g, mem_up[j])))
    for j in range(1, ng):
        pl.when(g + j < ng)(lambda j=j: greet(barrier, (grp_up[j], m)))

    own_g = pltpu.make_async_copy(pts_hbm, gp.at[m], loc_sem.at[0])
    own_c = pltpu.make_async_copy(pts_hbm, cp.at[g], loc_sem.at[1])
    own_g.start()
    own_c.start()
    slab_copy = pltpu.make_async_copy(slab_hbm, slab_v, slab_sem)
    slab_copy.start()
    pad = cp.shape[0] - ng
    if pad:
        cp[pl.ds(ng, pad)] = jnp.zeros((pad, owned, width), jnp.float32)

    pl.when(m + g > 0)(lambda: pl.semaphore_wait(barrier, m + g))
    for j in reversed(range(1, nm)):
        pl.when(m >= j)(lambda j=j: greet(ready.at[j - 1], (g, mem_down[j])))
    for j in reversed(range(1, ng)):
        pl.when(g >= j)(lambda j=j: greet(cready.at[j - 1], (grp_down[j], m)))

    def remote(src, dst, send_sem, recv_sem, device):
        return pltpu.make_async_remote_copy(
            src_ref=src, dst_ref=dst, send_sem=send_sem, recv_sem=recv_sem,
            device_id=device, device_id_type=MESH,
        )

    def own_up(j):
        return remote(pts_hbm, gp.at[m], gsend.at[j - 1], grecv.at[j - 1], (g, mem_up[j]))

    def own_down(j):
        d = nm - j
        return remote(pts_hbm, gp.at[m], gsend.at[d - 1], grecv.at[d - 1], (g, mem_down[j]))

    def pass_up(back, j, slot):
        block = gp.at[mem_down[back]]
        return remote(block, block, psend.at[slot], grecv.at[back + j - 1], (g, mem_up[j]))

    def pair_up(j):
        return remote(pts_hbm, cp.at[g], csend, crecv, (grp_up[j], m))

    def pair_down(j):
        return remote(pts_hbm, cp.at[g], csend, crecv, (grp_down[j], m))

    def take(owner, d):
        block = gp.at[owner]
        pltpu.make_async_copy(block, block, grecv.at[d - 1]).wait()

    sent = []

    def send(cond, make, *args):
        pl.when(cond)(lambda: make(*args).start())
        sent.append((cond, make, args))

    for j in reversed(range(1, nm)):
        send(m >= j, own_down, j)
    for j in range(1, ng):
        pl.when(g >= j)(lambda j=j: pair_down(j).start())

    early_mate = both(odd, m + 2 < nm)
    early_pass = both(odd, m >= 3, m + 3 < nm)
    slot = 1
    for j in range(1, nm):
        pl.when(m + j < nm)(lambda j=j: pl.semaphore_wait(ready.at[j - 1], 1))
        if j in (1, 2, 4):
            send(m + j < nm, own_up, j)
        elif j == 3:
            send(both(odd, m + j < nm), own_up, j)
        elif j == 5:
            send(both(even, m + j < nm), own_up, j)
        if j == 2:
            pl.when(early_mate)(lambda: take(mem_down[1], 1))
            send(early_mate, pass_up, 1, 2, 0)
        if j == 3:
            @pl.when(early_pass)
            def _():
                take(mem_down[2], 2)
                take(mem_down[3], 3)
        if 3 <= j < nm - 3:
            for back in (3, 2):
                send(both(early_pass, m + j < nm), pass_up, back, j, slot)
                slot += 1
    for k in range(1, ng):
        pl.when(g + k < ng)(lambda k=k: pl.semaphore_wait(cready.at[k - 1], 1))
        pl.when(g + k < ng)(lambda k=k: pair_up(k).start())

    slab_copy.wait()
    for c in range(n_chunk):
        part = pl.ds(c * chunk, chunk)
        b12[part], b31[part], bn[:, part] = prep_rows(slab_v[part])
    own_g.wait()
    own_c.wait()
    pair_blocks = cp.at[pl.ds(0, ng - 1)]
    pltpu.make_async_copy(pair_blocks, pair_blocks, crecv).wait()
    pair_rows = cp[...].reshape(cp.shape[0] * owned, width)
    pair12, pair31, pair_norms = prep_rows(pair_rows)

    def row_of(part):
        short = -part.shape[0] % LANES
        if short:
            part = jnp.concatenate([part, jnp.zeros((short, LANES), jnp.float32)], axis=0)
        return jnp.sum(part.T, axis=0, keepdims=True)

    def folded(w):
        total = w[:, :LANES]
        for k in range(1, w.shape[1] // LANES):
            total = total + w[:, k * LANES:(k + 1) * LANES]
        return total

    def accum(w, r12):
        return jnp.dot(
            jnp.concatenate(split2(w), axis=0), r12, preferred_element_type=jnp.float32
        )

    def partial_sums(first, blocks):
        for owner in range(first, first + blocks):
            d = lax.rem(m - owner + nm, nm)
            waited = jnp.logical_or(
                both(early_mate, d == 1), both(early_pass, jnp.logical_or(d == 2, d == 3))
            )
            pl.when(both(d > 0, jnp.logical_not(waited)))(
                lambda owner=owner, d=d: take(owner, jnp.maximum(d, 1))
            )
        count = blocks * owned
        pts = gp[first:first + blocks].reshape(count, width)
        norm1 = jnp.sum(pts * pts, axis=1, keepdims=True) + 1.0
        p1, p2, p3 = split3(-2.0 * pts)
        left12 = jnp.concatenate(
            [jnp.concatenate([p1, p1], axis=1), jnp.concatenate([p2, p2], axis=1)], axis=0
        )
        left31 = jnp.concatenate([p1, p3], axis=1)

        def weights(r12, r31, norms):
            twice = ndot(left12, r12)
            cross = twice[:count] + twice[count:] + ndot(left31, r31)
            return lax.rsqrt(norm1 + norms + cross)

        w = weights(pair12, pair31, pair_norms[0:1])
        if pad:
            lane = lax.broadcasted_iota(jnp.int32, w.shape, 1)
            w = jnp.where(lane < ng * owned, w, 0.0)
        pair_part = folded(w)
        acc = accum(w * (-ratio), pair12)
        weight_part = None
        for c in range(n_chunk):
            part = pl.ds(c * chunk, chunk)
            r12 = b12[part]
            w = weights(r12, b31[part], bn[0:1, part])
            weight_part = folded(w) if weight_part is None else weight_part + folded(w)
            acc = acc + accum(w, r12)
        acc = acc[:count] + acc[count:]
        acc = acc[:, :width] + acc[:, width:]
        weight_row = row_of(weight_part)
        pair_row = row_of(pair_part)
        for b in range(blocks):
            t = first + b
            lo = (b * owned) // LANES * LANES
            sendbuf[t, 0:owned] = acc[b * owned:(b + 1) * owned]
            sendbuf[t, owned:owned + 1] = weight_row[:, lo:lo + LANES]
            sendbuf[t, owned + 1:owned + 2] = pair_row[:, lo:lo + LANES]
        for t in range(first, first + blocks):
            slot = lax.rem(t - m + nm, nm)
            pl.when(slot > 0)(lambda t=t, slot=slot: remote(
                sendbuf.at[t, pl.ds(0, owned + 2)], recvbuf.at[slot, pl.ds(0, owned + 2)],
                rsend, rrecv, (g, t),
            ).start())

    lead = min(LEAD, nm)
    if lead:
        partial_sums(0, lead)
    partial_sums(lead, nm - lead)

    filled = recvbuf.at[pl.ds(1, nm - 1), pl.ds(0, owned + 2)]
    pltpu.make_async_copy(filled, filled, rrecv).wait()
    vec = sendbuf[m, 0:owned]
    sums = sendbuf[m, owned:owned + 2]
    for j in range(1, nm):
        vec = vec + recvbuf[j, 0:owned]
        sums = sums + recvbuf[j, owned:owned + 2]
    lane = lax.broadcasted_iota(jnp.int32, (owned, LANES), 1)
    row = lax.broadcasted_iota(jnp.int32, (owned, LANES), 0)
    place = jnp.where(m < lead, m, m - lead)
    mine = lane == row + lax.rem(place * owned, LANES)
    weight = jnp.sum(jnp.where(mine, sums[0:1], 0.0), axis=1, keepdims=True)
    pair = jnp.sum(jnp.where(mine, sums[1:2], 0.0), axis=1, keepdims=True)
    out_ref[...] = (gp[m] * (ratio * pair) + vec) / weight
    pltpu.make_async_copy(filled, filled, rsend).wait()
    pltpu.make_async_copy(pair_blocks, pair_blocks, csend).wait()
    for cond, make, args in sent:
        pl.when(cond)(lambda make=make, args=args: make(*args).wait_send())


def shards(points, slab):
    owned, width = points.shape
    rows = slab.shape[0]
    ng, nm = lax.axis_size("grp"), lax.axis_size("mem")
    ratio = rows / (owned * ng)
    chunk = min(rows, 512)
    pair_slots = -(-ng * owned // LANES) * LANES // owned
    sem = pltpu.SemaphoreType.DMA
    return pl.pallas_call(
        functools.partial(kernel, ng, nm, ratio, chunk),
        out_shape=pltpu.VMEM((owned, width), jnp.float32),
        in_specs=[pl.BlockSpec(memory_space=pl.ANY)] * 2,
        out_specs=pl.BlockSpec(memory_space=pltpu.VMEM),
        scratch_shapes=[
            pltpu.VMEM((nm, owned, width), jnp.float32),
            pltpu.VMEM((pair_slots, owned, width), jnp.float32),
            pltpu.VMEM((rows, width), jnp.float32),
            pltpu.VMEM((rows, 2 * width), jnp.bfloat16),
            pltpu.VMEM((rows, 2 * width), jnp.bfloat16),
            pltpu.VMEM((8, rows), jnp.float32),
            pltpu.VMEM((nm, owned + 8, width), jnp.float32),
            pltpu.VMEM((nm, owned + 8, width), jnp.float32),
            sem((2,)), sem,
            pltpu.SemaphoreType.REGULAR((nm - 1,)), pltpu.SemaphoreType.REGULAR((ng - 1,)),
            sem((nm - 1,)), sem((nm - 1,)), sem((max(1, 1 + 2 * (nm - 6)),)),
            sem, sem, sem, sem,
        ],
        compiler_params=pltpu.CompilerParams(collective_id=0, has_side_effects=True),
    )(points, slab)


def solution(mesh):
    placed = (P(("grp", "mem"), None), P("mem", None))
    return jax.shard_map(
        shards, mesh=mesh, in_specs=placed, out_specs=P(("grp", "mem"), None), check_vma=False
    )
```

time: 16.5 us -> 14.5 us (0.88)
  Pallas kernels: 15 us -> 13.7 us
  local copies, waits for them, and re-layouts: 1.3 us -> 0.6 us
    pallas_call x1, Pallas kernels: 15 us -> 13.7 us  [shards(): pl.pallas_call(functools.partial(kernel, ng, nm, ratio, chunk), out_shape...]
    unnamed x1, local copies, waits for them, and re-layouts: 1.3 us -> 0.6 us
where the time goes in v2:
time: 14.5 us; the launch traced here: 14.3 us
  Pallas kernels  13.7 us (94%)
  local copies, waits for them, and re-layouts  0.6 us (4%)
    pallas_call x1, Pallas kernels, shards(): pl.pallas_call(functools.partial(kernel, ng, nm, ratio, chunk), out_shape...  13.7 us
    unnamed x1, local copies, waits for them, and re-layouts  0.6 us

profile of v2, /device:TPU:0, one launch (start us, length us, event | category | flops | bytes accessed | tf_op | source)
XLA Modules:
  0.0 14.3 jit_solution(14494501381156002862)
XLA Ops:
  0.0 13.7 %shard_map.28 = f32[16,128]{1,0:T(8,128)S(1)} custom-call(f32[16,128]{1,0:T(8,128)} %pts_hbm.1, f32[2048,128]{1,0:T(8,128)} %slab_hbm.1), custom_call_target="tpu_custom_call" | custom-call | tf_op jit(solution)/shard_map/pallas_call | solution.py:270
  13.7 0.6 %copy.4 = f32[16,128]{1,0:T(8,128)} copy(f32[16,128]{1,0:T(8,128)S(1)} %shard_map.28) | data formatting | bytes 16384

commit v3 on v2

--- a/solution.py
+++ b/solution.py
@@ -211,12 +211,11 @@
         pair_part = folded(w)
         acc = accum(w * (-ratio), pair12)
         weight_part = None
-        for c in range(n_chunk):
-            part = pl.ds(c * chunk, chunk)
-            r12 = b12[part]
-            w = weights(r12, b31[part], bn[0:1, part])
+        parts = [pl.ds(c * chunk, chunk) for c in range(n_chunk)]
+        all_w = [weights(b12[part], b31[part], bn[0:1, part]) for part in parts]
+        for w, part in zip(all_w, parts):
             weight_part = folded(w) if weight_part is None else weight_part + folded(w)
-            acc = acc + accum(w, r12)
+            acc = acc + accum(w, b12[part])
         acc = acc[:count] + acc[count:]
         acc = acc[:, :width] + acc[:, width:]
         weight_row = row_of(weight_part)
@@ -264,7 +263,7 @@
     rows = slab.shape[0]
     ng, nm = lax.axis_size("grp"), lax.axis_size("mem")
     ratio = rows / (owned * ng)
-    chunk = min(rows, 512)
+    chunk = min(rows, 256)
     pair_slots = -(-ng * owned // LANES) * LANES // owned
     sem = pltpu.SemaphoreType.DMA
     return pl.pallas_call(

time: 14.5 us -> 14.3 us (0.986)
  Pallas kernels: 13.7 us -> 13.5 us
    pallas_call x1, Pallas kernels: 13.7 us -> 13.5 us  [shards(): pl.pallas_call(functools.partial(kernel, ng, nm, ratio, chunk), out_shape...]
where the time goes in v3:
time: 14.3 us; the launch traced here: 14.1 us
  Pallas kernels  13.5 us (94%)
  local copies, waits for them, and re-layouts  0.6 us (4%)
    pallas_call x1, Pallas kernels, shards(): pl.pallas_call(functools.partial(kernel, ng, nm, ratio, chunk), out_shape...  13.5 us
    unnamed x1, local copies, waits for them, and re-layouts  0.6 us

profile of v3, /device:TPU:0, one launch (start us, length us, event | category | flops | bytes accessed | tf_op | source)
XLA Modules:
  0.0 14.1 jit_solution(10607424618444005059)
XLA Ops:
  0.0 13.5 %shard_map.28 = f32[16,128]{1,0:T(8,128)S(1)} custom-call(f32[16,128]{1,0:T(8,128)} %pts_hbm.1, f32[2048,128]{1,0:T(8,128)} %slab_hbm.1), custom_call_target="tpu_custom_call" | custom-call | tf_op jit(solution)/shard_map/pallas_call | solution.py:269
  13.5 0.6 %copy.4 = f32[16,128]{1,0:T(8,128)} copy(f32[16,128]{1,0:T(8,128)S(1)} %shard_map.28) | data formatting | bytes 16384
